TPU v7x, 512 devices: a whole 4x8x8 slice. The times are simulated.
512 devices in a mesh: tile: 32 (over y, x), ir: 16 (over z, core).
Axes of the slice: x: 4, y: 8, z: 8, core: 2. Of those that a mesh axis runs over, the one named last changes fastest.
Arguments:
- samples: bfloat16 [4096, 1024], P(('tile', 'ir')), may hold values from -6 to 6
- ir_spectra: bfloat16 [16, 128, 2, 1024], P(None, 'ir'), may hold values from -0.5 to 0.5
- clip_lengths: int32 [16], replicated, may hold values from 1 to 1024, 4096 in all
- room_ids: int32 [16], replicated, may hold values from 0 to 15
Outputs:
- filtered: float32 [4096, 1024], P(('tile', 'ir'))
Inputs may be any that keep to these rules, and one draw needn't show every extreme that they name: `clip_lengths`: the lengths sum to 4096; clips lie end to end in block order.
All inputs are finite; a program needn't handle non-finite values.
Results may differ from a plain program's by a relative error of at most 0.0037.
Values may be sent and summed in bfloat16 or wider, within the bound.
A program may use at most 128 MiB of HBM per device.

v0:
```python
import jax
import jax.numpy as jnp
import numpy as np
from jax import lax
from jax.sharding import PartitionSpec as P


def from_behind(x, axis, by):
    length = lax.axis_size(axis)
    pairs = [(i, i + by) for i in range(length) if 0 <= i + by < length]
    return lax.ppermute(x, axis, pairs)


def in_blocks(x, dim, length):
    before, after = (x.shape[:dim], x.shape[dim + 1 :])
    return jnp.moveaxis(x.reshape(*before, length, -1, *after), dim, 0)


def sent_and_summed(x, axis, dim):
    tiles = in_blocks(x, dim, lax.axis_size(axis))
    arrived = lax.all_to_all(tiles, axis, split_axis=0, concat_axis=0, tiled=True)
    return arrived.sum(axis=0)


def forward_table(width):
    length = 2 * width
    sample = np.arange(length)
    bins = np.arange(width)
    phase = sample[:, None] * bins[None, :] % length
    angle = phase * (2.0 * np.pi / length)
    parity = np.where(sample % 2 == 0, 1.0, -1.0)
    sines = np.where(bins[None, :] == 0, parity[:, None], -np.sin(angle))
    table = np.concatenate([np.cos(angle), sines], axis=1)
    return jnp.asarray(table, dtype=jnp.float32).astype(jnp.bfloat16)


def inverse_table(width):
    length = 2 * width
    bins = np.arange(width)
    outputs = width + np.arange(width)
    phase = bins[:, None] * outputs[None, :] % length
    angle = phase * (2.0 * np.pi / length)
    weight = np.where(bins == 0, 1.0, 2.0)[:, None] / length
    parity = np.where(outputs % 2 == 0, 1.0, -1.0)[None, :] / length
    cosines = weight * np.cos(angle)
    sines = np.where(bins[:, None] == 0, parity, -weight * np.sin(angle))
    table = np.concatenate([cosines, sines], axis=0)
    return jnp.asarray(table, dtype=jnp.float32)


def packed_product(spectrum, response, width):
    are, aim = (spectrum[:, :width], spectrum[:, width:])
    hre, him = (response[:, :width], response[:, width:])
    cross = (jnp.arange(width, dtype=jnp.int32) > 0).astype(jnp.float32)[None, :]
    real = are * hre - cross * aim * him
    imag = cross * (are * him + aim * hre) + (1.0 - cross) * aim * him
    return jnp.concatenate([real, imag], axis=1)


def clip_info(clip_lengths, room_ids, blocks):
    ends = jnp.cumsum(clip_lengths)
    starts = ends - clip_lengths
    member = (blocks[:, None] >= starts[None, :]) & (blocks[:, None] < ends[None, :])
    begin = jnp.sum(jnp.where(member, starts[None, :], 0), axis=1)
    room = jnp.sum(jnp.where(member, room_ids[None, :], 0), axis=1)
    return (begin, room)


def on_device(samples, ir_spectra, clip_lengths, room_ids):
    rows, width = samples.shape
    groups = lax.axis_size("ir")
    count = rows * groups
    rooms, part_dev = (ir_spectra.shape[0], ir_spectra.shape[1])
    parts = part_dev * groups
    tile_base = lax.axis_index("tile") * count
    own_blocks = tile_base + lax.axis_index("ir") * rows + jnp.arange(rows, dtype=jnp.int32)
    own_begin, own_room = clip_info(clip_lengths, room_ids, own_blocks)
    before = from_behind(samples[rows - 1 :], ("tile", "ir"), 1)
    earlier = jnp.concatenate([before, samples[:-1]], axis=0)
    earlier = jnp.where((own_blocks == own_begin)[:, None], jnp.zeros_like(earlier), earlier)
    frames = jnp.concatenate([earlier, samples], axis=1)
    own_spectra = jnp.dot(frames, forward_table(width), preferred_element_type=jnp.float32).astype(
        jnp.bfloat16
    )
    blocks = tile_base + jnp.arange(count, dtype=jnp.int32)
    begin, room = clip_info(clip_lengths, room_ids, blocks)
    room_hot = (room[:, None] == jnp.arange(rooms, dtype=jnp.int32)[None, :]).astype(jnp.bfloat16)
    inverse = inverse_table(width)
    spectra = lax.all_gather(own_spectra, "ir", axis=0, tiled=True)
    delayed = from_behind(spectra[count - (parts - 1) :], "tile", 1)
    padded = jnp.concatenate([delayed, spectra], axis=0)
    flat_filters = ir_spectra.reshape(rooms, part_dev * 2 * width)
    selected = jnp.dot(room_hot, flat_filters, preferred_element_type=jnp.float32).astype(
        jnp.bfloat16
    )
    selected = selected.reshape(count, part_dev, 2 * width)
    first = lax.axis_index("ir") * part_dev

    def add_partition(index, summed):
        delay = first + index
        moved = lax.dynamic_slice_in_dim(padded, parts - 1 - delay, count, 0)
        chosen = lax.dynamic_index_in_dim(selected, index, 1, keepdims=False)
        live = blocks - delay >= begin
        term = packed_product(moved.astype(jnp.float32), chosen.astype(jnp.float32), width)
        return summed + jnp.where(live[:, None], term, jnp.zeros_like(term))

    summed = lax.fori_loop(0, part_dev, add_partition, jnp.zeros((count, 2 * width), jnp.float32))
    return sent_and_summed(
        jnp.dot(
            summed, inverse, precision=lax.Precision.HIGHEST, preferred_element_type=jnp.float32
        ),
        "ir",
        0,
    )


def solution(mesh):
    in_specs = (P(("tile", "ir"), None), P(None, "ir", None, None), P(), P())
    out_specs = P(("tile", "ir"), None)
    return jax.shard_map(
        on_device, mesh=mesh, in_specs=in_specs, out_specs=out_specs, check_vma=False
    )
```

profile of v0, /device:TPU:33, one launch (start us, length us, event | category | flops | bytes accessed | tf_op | source)
XLA Modules:
  0.0 97.9 jit_solution(4870245839410674996)
XLA Ops:
  0.0 0.8 slice.49
  0.8 4.5 %collective-permute-start = (bf16[1,1024]{1,0:T(2,128)(2,1)S(1)}, bf16[1,1024]{1,0:T(2,128)(2,1)S(1)}, u32[]{:S(2)}, u32[]{:S(2)}) collective-permute-start(bf16[1,1024]{1,0:T(2,128)(2,1)S(1)} %slice.49), channel_id=1, source_target_pairs={{0,1},{1,2},{2,3},{3,4},{4,5},{5,6},{6,7},{7,8},{8,9},{9,10},{10,1... | collective-permute-start | bytes 6152 | tf_op jit(solution)/shard_map/ppermute | solution.py:11
  5.4 0.7 copy.11
  6.3 0.7 sub.58
  6.9 2.8 %convolution_bitcast_fusion = f32[8,2048]{1,0:T(8,128)S(1)} fusion(bf16[1024,2048]{1,0:T(8,128)(2,1)} %constant.107, bf16[8,1024]{1,0:T(8,128)(2,1)} %param.8), kind=kOutput, calls=%fused_computation.14 | convolution fusion | flops 33554432 | bytes 4276224 | tf_op jit(solution)/shard_map/dot_general | solution.py:82
  10.0 0.4 reshape.73
  10.4 2.9 %fusion.5 = bf16[8,2048]{1,0:T(8,128)(2,1)S(1)} fusion(f32[8,2048]{1,0:T(8,128)S(1)} %convolution_bitcast_fusion, bf16[1024,2048]{1,0:T(8,128)(2,1)} %constant.106, bf16[7,1024]{1,0:T(8,128)(2,1)S(1)} %bitcast.23, bf16[1,1024]{1,0:T(2,128)(2,1)S(1)} %collective-permute-done, pred[8]{0:T(512)(128)(4,1)S(1)} %fusion.13), kind=kOutput, calls=%fused_computation.16 | convolution fusion | flops 33628160 | bytes 4309000 | tf_op jit(solution)/shard_map/dot_general | solution.py:82
  13.3 22.5 %all_gather.3 = bf16[128,2048]{1,0:T(8,128)(2,1)S(1)} all-gather(bf16[8,2048]{1,0:T(8,128)(2,1)S(1)} %fusion.5), channel_id=1, replica_groups=mesh['tile'=32,'ir'=16] {'ir'}, dimensions={0}, use_global_device_ids=true | all-gather | bytes 557056 | tf_op jit(solution)/shard_map/all_gather | solution.py:89
  35.9 3.1 %collective-permute-start.1 = (bf16[127,2048]{1,0:T(8,128)(2,1)S(1)}, bf16[127,2048]{1,0:T(8,128)(2,1)S(1)}, u32[]{:S(2)}, u32[]{:S(2)}) collective-permute-start(bf16[127,2048]{1,0:T(8,128)(2,1)S(1)} %slice.62), channel_id=1, source_target_pairs={{0,16},{16,32},{32,48},{48,64},{64,80},{80,96},{96,112},{112,128},... | collective-permute-start | bytes 1560584 | tf_op jit(solution)/shard_map/ppermute | solution.py:11
  39.1 1.3 %convolution_convert_fusion = bf16[128,16384]{1,0:T(8,128)(2,1)S(1)} fusion(bf16[16,16384]{1,0:T(8,128)(2,1)S(1)} %reshape.73, s32[128]{0:T(128)S(1)} %get-tuple-element.230), kind=kOutput, calls=%fused_computation.12 | convolution fusion | flops 69208064 | bytes 4719104 | tf_op jit(solution)/shard_map/dot_general | solution.py:93
  40.4 2.2 %copy.15 = bf16[16,8,8,2048]{3,2,0,1:T(8,128)(2,1)} copy(bf16[16,8,8,2048]{3,2,1,0:T(8,128)(2,1)S(1)} %bitcast.21) | data formatting | bytes 8388608 | tf_op jit(solution)/shard_map/reshape | solution.py:96
  42.6 11.8 %collective-permute-done.1 = bf16[127,2048]{1,0:T(8,128)(2,1)S(1)} collective-permute-done((bf16[127,2048]{1,0:T(8,128)(2,1)S(1)}, bf16[127,2048]{1,0:T(8,128)(2,1)S(1)}, u32[]{:S(2)}, u32[]{:S(2)}) %collective-permute-start.1) | collective-permute-done | bytes 520224 | tf_op jit(solution)/shard_map/ppermute | solution.py:11
  54.5 14.4 %while.16 = (s32[]{:T(128)}, f32[128,2048]{1,0:T(8,128)S(1)}, s32[]{:T(128)}, s32[128]{0:T(128)S(1)}, bf16[255,2048]{1,0:T(8,128)(2,1)S(1)}, /*index=5*/bf16[128...) while((s32[]{:T(128)}, f32[128,2048]{1,0:T(8,128)S(1)}, ...), condition=%wide.region_5.6_spmd.clone, body=%wide.region_4.5_spmd.clone.sunk | while | flops 3020168 | bytes 9454529 | solution.py:107
  54.7 1.1 %bitcast_convert_fusion.2 = f32[128,2048]{1,0:T(8,128)S(1)} fusion(bf16[128,8,2048]{2,0,1:T(8,128)(2,1)} %get-tuple-element.322, s32[]{:T(128)} %get-tuple-element.306), kind=kLoop, calls=%fused_computation.3.clone.1 | loop fusion | flops 262144 | bytes 1572868 | tf_op jit(solution)/shard_map/while/body/eval_jaxpr/convert_element_type | solution.py:104
  56.5 1.1 %bitcast_convert_fusion.2 = f32[128,2048]{1,0:T(8,128)S(1)} fusion(bf16[128,8,2048]{2,0,1:T(8,128)(2,1)} %get-tuple-element.322, s32[]{:T(128)} %get-tuple-element.306), kind=kLoop, calls=%fused_computation.3.clone.1 | loop fusion | flops 262144 | bytes 1572868 | tf_op jit(solution)/shard_map/while/body/eval_jaxpr/convert_element_type | solution.py:104
  58.3 1.1 %bitcast_convert_fusion.2 = f32[128,2048]{1,0:T(8,128)S(1)} fusion(bf16[128,8,2048]{2,0,1:T(8,128)(2,1)} %get-tuple-element.322, s32[]{:T(128)} %get-tuple-element.306), kind=kLoop, calls=%fused_computation.3.clone.1 | loop fusion | flops 262144 | bytes 1572868 | tf_op jit(solution)/shard_map/while/body/eval_jaxpr/convert_element_type | solution.py:104
  60.1 1.1 %bitcast_convert_fusion.2 = f32[128,2048]{1,0:T(8,128)S(1)} fusion(bf16[128,8,2048]{2,0,1:T(8,128)(2,1)} %get-tuple-element.322, s32[]{:T(128)} %get-tuple-element.306), kind=kLoop, calls=%fused_computation.3.clone.1 | loop fusion | flops 262144 | bytes 1572868 | tf_op jit(solution)/shard_map/while/body/eval_jaxpr/convert_element_type | solution.py:104
  61.9 1.1 %bitcast_convert_fusion.2 = f32[128,2048]{1,0:T(8,128)S(1)} fusion(bf16[128,8,2048]{2,0,1:T(8,128)(2,1)} %get-tuple-element.322, s32[]{:T(128)} %get-tuple-element.306), kind=kLoop, calls=%fused_computation.3.clone.1 | loop fusion | flops 262144 | bytes 1572868 | tf_op jit(solution)/shard_map/while/body/eval_jaxpr/convert_element_type | solution.py:104
  63.7 1.1 %bitcast_convert_fusion.2 = f32[128,2048]{1,0:T(8,128)S(1)} fusion(bf16[128,8,2048]{2,0,1:T(8,128)(2,1)} %get-tuple-element.322, s32[]{:T(128)} %get-tuple-element.306), kind=kLoop, calls=%fused_computation.3.clone.1 | loop fusion | flops 262144 | bytes 1572868 | tf_op jit(solution)/shard_map/while/body/eval_jaxpr/convert_element_type | solution.py:104
  65.5 1.1 %bitcast_convert_fusion.2 = f32[128,2048]{1,0:T(8,128)S(1)} fusion(bf16[128,8,2048]{2,0,1:T(8,128)(2,1)} %get-tuple-element.322, s32[]{:T(128)} %get-tuple-element.306), kind=kLoop, calls=%fused_computation.3.clone.1 | loop fusion | flops 262144 | bytes 1572868 | tf_op jit(solution)/shard_map/while/body/eval_jaxpr/convert_element_type | solution.py:104
  67.3 1.1 %bitcast_convert_fusion.2 = f32[128,2048]{1,0:T(8,128)S(1)} fusion(bf16[128,8,2048]{2,0,1:T(8,128)(2,1)} %get-tuple-element.322, s32[]{:T(128)} %get-tuple-element.306), kind=kLoop, calls=%fused_computation.3.clone.1 | loop fusion | flops 262144 | bytes 1572868 | tf_op jit(solution)/shard_map/while/body/eval_jaxpr/convert_element_type | solution.py:104
  68.9 7.2 %convolution_bitcast_fusion.1 = f32[16,8,1024]{2,1,0:T(8,128)S(1)} fusion(f32[128,2048]{1,0:T(8,128)S(1)} %get-tuple-element.181, f32[2048,1024]{1,0:T(8,128)} %constant.102.clone), kind=kOutput, calls=%fused_computation.17 | convolution fusion | flops 3221225472 | bytes 9961472 | tf_op jit(solution)/shard_map/dot_general | solution.py:109
  76.2 21.1 %all_to_all.5 = f32[16,8,1024]{2,1,0:T(8,128)S(1)} all-to-all(f32[16,8,1024]{2,1,0:T(8,128)S(1)} %convolution_bitcast_fusion.1), channel_id=1, replica_groups=mesh['tile'=32,'ir'=16] {'ir'}, dimensions={0} | all-to-all | bytes 1048576 | tf_op jit(solution)/shard_map/all_to_all | solution.py:21
  97.3 0.6 reduce_sum.39
  (65 shorter events, 5.4 us)
Async XLA Ops:
  0.0 10.4 %copy-start.1 = (bf16[8,1024]{1,0:T(8,128)(2,1)S(1)}, bf16[8,1024]{1,0:T(8,128)(2,1)}, u32[]{:S(2)}) copy-start(bf16[8,1024]{1,0:T(8,128)(2,1)} %param.8) | copy-start | bytes 49156
  0.0 10.0 %copy-start = (bf16[16,8,2,1024]{3,2,1,0:T(2,128)(2,1)S(1)}, bf16[16,8,2,1024]{3,2,1,0:T(2,128)(2,1)}, u32[]{:S(2)}) copy-start(bf16[16,8,2,1024]{3,2,1,0:T(2,128)(2,1)} %param.9) | copy-start | bytes 1572868
  0.8 9.6 %collective-permute-start = (bf16[1,1024]{1,0:T(2,128)(2,1)S(1)}, bf16[1,1024]{1,0:T(2,128)(2,1)S(1)}, u32[]{:S(2)}, u32[]{:S(2)}) collective-permute-start(bf16[1,1024]{1,0:T(2,128)(2,1)S(1)} %slice.49), channel_id=1, source_target_pairs={{0,1},{1,2},{2,3},{3,4},{4,5},{5,6},{6,7},{7,8},{8,9},{9,10},{10,1... | collective-permute-start | bytes 6152 | tf_op jit(solution)/shard_map/ppermute | solution.py:11
  9.8 29.2 %copy-start.2 = (s32[16]{0:T(128)S(1)}, s32[16]{0:T(128)}, u32[]{:S(2)}) copy-start(s32[16]{0:T(128)} %param.11) | copy-start | bytes 196
  35.9 18.5 %collective-permute-start.1 = (bf16[127,2048]{1,0:T(8,128)(2,1)S(1)}, bf16[127,2048]{1,0:T(8,128)(2,1)S(1)}, u32[]{:S(2)}, u32[]{:S(2)}) collective-permute-start(bf16[127,2048]{1,0:T(8,128)(2,1)S(1)} %slice.62), channel_id=1, source_target_pairs={{0,16},{16,32},{32,48},{48,64},{64,80},{80,96},{96,112},{112,128},... | collective-permute-start | bytes 1560584 | tf_op jit(solution)/shard_map/ppermute | solution.py:11
where the time goes:
time: 98.5 us; the launch traced here: 97.9 us
  blocking collectives  43.6 us (44%)
  other arithmetic  15.7 us (16%)
  matrix products  14.2 us (14%)
  waiting for transfers between devices  11.8 us (12%)
  starting transfers between devices  7.67 us (8%)
  local copies, waits for them, and re-layouts  4.29 us (4%)
    all_gather x1, blocking collectives, on_device(): spectra = lax.all_gather(own_spectra, 'ir', axis=0, tiled=True)  22.5 us
    all_to_all x1, blocking collectives, sent_and_summed(): lax.all_to_all(tiles, axis, split_axis=0, concat_axis=0, tiled=True)  21.1 us
    ppermute x2, waiting for transfers between devices, from_behind(): return lax.ppermute(x, axis, pairs)  11.8 us
    convert_element_type x8, other arithmetic, add_partition(): chosen.astype(jnp.float32)  9.15 us
    ppermute x2, starting transfers between devices, from_behind(): return lax.ppermute(x, axis, pairs)  7.67 us
    dot_general x1, matrix products, on_device(): jnp.dot(summed, inverse, precision=lax.Precision.HIGHEST, preferred_eleme...  7.21 us
    dot_general x2, matrix products, on_device(): jnp.dot(frames, forward_table(width), preferred_element_type=jnp.float32)  5.72 us
    reshape x1, local copies, waits for them, and re-layouts, on_device(): selected = selected.reshape(count, part_dev, 2 * width)  2.23 us
  transfers between devices with their start and end apart: 2, of which 1 were waited for; matrix products, arithmetic and copies ran while one was open for 9% of the time, Pallas kernels for 0%

commit v1 on v0

--- a/solution.py
+++ b/solution.py
@@ -86,7 +86,21 @@
     begin, room = clip_info(clip_lengths, room_ids, blocks)
     room_hot = (room[:, None] == jnp.arange(rooms, dtype=jnp.int32)[None, :]).astype(jnp.bfloat16)
     inverse = inverse_table(width)
-    spectra = lax.all_gather(own_spectra, "ir", axis=0, tiled=True)
+    ways, here, step = (lax.axis_size("ir"), lax.axis_index("ir"), own_spectra.shape[0])
+    shape = [n * ways if d == 0 else n for d, n in enumerate(own_spectra.shape)]
+    full = lax.dynamic_update_slice_in_dim(
+        jnp.zeros(shape, own_spectra.dtype), own_spectra, here * step, axis=0
+    )
+    going_up = going_down = own_spectra
+    for far in range(1, ways // 2 + 1):
+        going_up = lax.ppermute(going_up, "ir", [(d, (d + 1) % ways) for d in range(ways)])
+        full = lax.dynamic_update_slice_in_dim(full, going_up, (here - far) % ways * step, axis=0)
+        if 2 * far < ways:
+            going_down = lax.ppermute(going_down, "ir", [(d, (d - 1) % ways) for d in range(ways)])
+            full = lax.dynamic_update_slice_in_dim(
+                full, going_down, (here + far) % ways * step, axis=0
+            )
+    spectra = full
     delayed = from_behind(spectra[count - (parts - 1) :], "tile", 1)
     padded = jnp.concatenate([delayed, spectra], axis=0)
     flat_filters = ir_spectra.reshape(rooms, part_dev * 2 * width)

time: 98.5 us -> 114 us (1.16)
  starting transfers between devices: 7.67 us -> 33.8 us
  blocking collectives: 43.6 us -> 24.9 us
  waiting for transfers between devices: 11.8 us -> 19.1 us
    ppermute x0 -> x15, starting transfers between devices: none -> 27.3 us  [the longest x7 27.3 us: on_device(): lax.ppermute(going_down, 'ir', [(d, (d - 1) % ways) for d in range(ways)])]
    all_gather x1 -> x0, blocking collectives: 22.5 us -> none  [on_device(): spectra = lax.all_gather(own_spectra, 'ir', axis=0, tiled=True)]
    ppermute x0 -> x15, waiting for transfers between devices: none -> 9.81 us  [the longest x8 8.67 us: on_device(): lax.ppermute(going_up, 'ir', [(d, (d + 1) % ways) for d in range(ways)])]
    all_to_all x1, blocking collectives: 21.1 us -> 24.9 us  [sent_and_summed(): lax.all_to_all(tiles, axis, split_axis=0, concat_axis=0, tiled=True)]
    ppermute x2, waiting for transfers between devices: 11.8 us -> 9.25 us  [from_behind(): return lax.ppermute(x, axis, pairs)]
    ppermute x2, starting transfers between devices: 7.67 us -> 6.47 us  [from_behind(): return lax.ppermute(x, axis, pairs)]
  transfers between devices with their start and end apart: 2 -> 17, of which waited for: 1 -> 16; matrix products, arithmetic and copies ran while one was open for 9% -> 8% of each run, Pallas kernels for 0% -> 0%
where the time goes in v1:
time: 114 us; the launch traced here: 113 us
  starting transfers between devices  33.8 us (30%)
  blocking collectives  24.9 us (22%)
  waiting for transfers between devices  19.1 us (17%)
  other arithmetic  15.8 us (14%)
  matrix products  14.3 us (13%)
  local copies, waits for them, and re-layouts  4.43 us (4%)
    ppermute x7, starting transfers between devices, on_device(): lax.ppermute(going_down, 'ir', [(d, (d - 1) % ways) for d in range(ways)])  27.3 us
    all_to_all x1, blocking collectives, sent_and_summed(): lax.all_to_all(tiles, axis, split_axis=0, concat_axis=0, tiled=True)  24.9 us
    ppermute x2, waiting for transfers between devices, from_behind(): return lax.ppermute(x, axis, pairs)  9.25 us
    convert_element_type x8, other arithmetic, add_partition(): chosen.astype(jnp.float32)  9.15 us
    ppermute x8, waiting for transfers between devices, on_device(): lax.ppermute(going_up, 'ir', [(d, (d + 1) % ways) for d in range(ways)])  8.67 us
    dot_general x1, matrix products, on_device(): jnp.dot(summed, inverse, precision=lax.Precision.HIGHEST, preferred_eleme...  7.21 us
    ppermute x2, starting transfers between devices, from_behind(): return lax.ppermute(x, axis, pairs)  6.47 us
    dot_general x2, matrix products, on_device(): jnp.dot(frames, forward_table(width), preferred_element_type=jnp.float32)  5.78 us
  transfers between devices with their start and end apart: 17, of which 16 were waited for; matrix products, arithmetic and copies ran while one was open for 8% of the time, Pallas kernels for 0%

profile of v1, /device:TPU:33, one launch (start us, length us, event | category | flops | bytes accessed | tf_op | source)
XLA Modules:
  0.0 113.1 jit_solution(3745484852829365856)
XLA Ops:
  0.8 4.5 %collective-permute-start = (bf16[1,1024]{1,0:T(2,128)(2,1)S(1)}, bf16[1,1024]{1,0:T(2,128)(2,1)S(1)}, u32[]{:S(2)}, u32[]{:S(2)}) collective-permute-start(bf16[1,1024]{1,0:T(2,128)(2,1)S(1)} %slice.49), channel_id=1, source_target_pairs={{0,1},{1,2},{2,3},{3,4},{4,5},{5,6},{6,7},{7,8},{8,9},{9,10},{10,1... | collective-permute-start | bytes 6152 | tf_op jit(solution)/shard_map/ppermute | solution.py:11
  6.9 2.9 %convolution_bitcast_fusion = f32[8,2048]{1,0:T(8,128)S(1)} fusion(bf16[1024,2048]{1,0:T(8,128)(2,1)} %constant.206, bf16[8,1024]{1,0:T(8,128)(2,1)} %param.8), kind=kOutput, calls=%fused_computation.14 | convolution fusion | flops 33554432 | bytes 4276224 | tf_op jit(solution)/shard_map/dot_general | solution.py:82
  10.1 2.9 %constant_dynamic-update-slice_fusion.15 = (bf16[128,2048]{1,0:T(8,128)(2,1)S(1)}, bf16[8,2048]{1,0:T(8,128)(2,1)S(1)}) fusion(bf16[128,2048]{1,0:T(8,128)(2,1)S(1)} %broadcast_in_dim.83, s32[]{:T(128)S(6)} %select_n.159, f32[8,2048]{1,0:T(8,128)S(1)} %convolution_bitcast_fusion, bf16[1024,2048]{1,0:T(8,128)(2,1)} %constant.205, ...), kind=kOutput, calls=%fused_computation.45 | convolution fusion | flops 33628160 | bytes 4346372 | tf_op jit(solution)/shard_map/dot_general | solution.py:82
  13.0 5.2 %collective-permute-start.2 = (bf16[8,2048]{1,0:T(8,128)(2,1)S(1)}, bf16[8,2048]{1,0:T(8,128)(2,1)S(1)}, u32[]{:S(2)}, u32[]{:S(2)}) collective-permute-start(bf16[8,2048]{1,0:T(8,128)(2,1)S(1)} %get-tuple-element.249), channel_id=1, source_target_pairs={{0,15},{1,0},{2,1},{3,2},{4,3},{5,4},{6,5},{7,6},{8,7},{9,8},{10,9... | collective-permute-start | bytes 98312 | tf_op jit(solution)/shard_map/ppermute | solution.py:99
  19.0 3.7 %collective-permute-start.4 = (bf16[8,2048]{1,0:T(8,128)(2,1)S(1)}, bf16[8,2048]{1,0:T(8,128)(2,1)S(1)}, u32[]{:S(2)}, u32[]{:S(2)}) collective-permute-start(bf16[8,2048]{1,0:T(8,128)(2,1)S(1)} %collective-permute-done.2), channel_id=1, source_target_pairs={{0,15},{1,0},{2,1},{3,2},{4,3},{5,4},{6,5},{7,6},{8,7},{9,8},{10,9... | collective-permute-start | bytes 98312 | tf_op jit(solution)/shard_map/ppermute | solution.py:99
  23.6 3.7 %collective-permute-start.6 = (bf16[8,2048]{1,0:T(8,128)(2,1)S(1)}, bf16[8,2048]{1,0:T(8,128)(2,1)S(1)}, u32[]{:S(2)}, u32[]{:S(2)}) collective-permute-start(bf16[8,2048]{1,0:T(8,128)(2,1)S(1)} %collective-permute-done.4), channel_id=1, source_target_pairs={{0,15},{1,0},{2,1},{3,2},{4,3},{5,4},{6,5},{7,6},{8,7},{9,8},{10,9... | collective-permute-start | bytes 98312 | tf_op jit(solution)/shard_map/ppermute | solution.py:99
  28.1 3.7 %collective-permute-start.8 = (bf16[8,2048]{1,0:T(8,128)(2,1)S(1)}, bf16[8,2048]{1,0:T(8,128)(2,1)S(1)}, u32[]{:S(2)}, u32[]{:S(2)}) collective-permute-start(bf16[8,2048]{1,0:T(8,128)(2,1)S(1)} %collective-permute-done.6), channel_id=1, source_target_pairs={{0,15},{1,0},{2,1},{3,2},{4,3},{5,4},{6,5},{7,6},{8,7},{9,8},{10,9... | collective-permute-start | bytes 98312 | tf_op jit(solution)/shard_map/ppermute | solution.py:99
  32.7 3.7 %collective-permute-start.10 = (bf16[8,2048]{1,0:T(8,128)(2,1)S(1)}, bf16[8,2048]{1,0:T(8,128)(2,1)S(1)}, u32[]{:S(2)}, u32[]{:S(2)}) collective-permute-start(bf16[8,2048]{1,0:T(8,128)(2,1)S(1)} %collective-permute-done.8), channel_id=1, source_target_pairs={{0,15},{1,0},{2,1},{3,2},{4,3},{5,4},{6,5},{7,6},{8,7},{9,8},{10,9... | collective-permute-start | bytes 98312 | tf_op jit(solution)/shard_map/ppermute | solution.py:99
  37.2 3.7 %collective-permute-start.12 = (bf16[8,2048]{1,0:T(8,128)(2,1)S(1)}, bf16[8,2048]{1,0:T(8,128)(2,1)S(1)}, u32[]{:S(2)}, u32[]{:S(2)}) collective-permute-start(bf16[8,2048]{1,0:T(8,128)(2,1)S(1)} %collective-permute-done.10), channel_id=1, source_target_pairs={{0,15},{1,0},{2,1},{3,2},{4,3},{5,4},{6,5},{7,6},{8,7},{9,8},{10,9... | collective-permute-start | bytes 98312 | tf_op jit(solution)/shard_map/ppermute | solution.py:99
  41.8 3.7 %collective-permute-start.14 = (bf16[8,2048]{1,0:T(8,128)(2,1)S(1)}, bf16[8,2048]{1,0:T(8,128)(2,1)S(1)}, u32[]{:S(2)}, u32[]{:S(2)}) collective-permute-start(bf16[8,2048]{1,0:T(8,128)(2,1)S(1)} %collective-permute-done.12), channel_id=1, source_target_pairs={{0,15},{1,0},{2,1},{3,2},{4,3},{5,4},{6,5},{7,6},{8,7},{9,8},{10,9... | collective-permute-start | bytes 98312 | tf_op jit(solution)/shard_map/ppermute | solution.py:99
  46.3 4.4 %collective-permute-done.15 = bf16[8,2048]{1,0:T(8,128)(2,1)S(1)} collective-permute-done((bf16[8,2048]{1,0:T(8,128)(2,1)S(1)}, bf16[8,2048]{1,0:T(8,128)(2,1)S(1)}, u32[]{:S(2)}, u32[]{:S(2)}) %collective-permute-start.15) | collective-permute-done | bytes 32800 | tf_op jit(solution)/shard_map/ppermute | solution.py:96
  50.9 1.9 %collective-permute-start.16 = (bf16[127,2048]{1,0:T(8,128)(2,1)S(1)}, bf16[127,2048]{1,0:T(8,128)(2,1)S(1)}, u32[]{:S(2)}, u32[]{:S(2)}) collective-permute-start(bf16[127,2048]{1,0:T(8,128)(2,1)S(1)} %slice.62), channel_id=1, source_target_pairs={{0,16},{16,32},{32,48},{48,64},{64,80},{80,96},{96,112},{112,128},... | collective-permute-start | bytes 1560584 | tf_op jit(solution)/shard_map/ppermute | solution.py:11
  52.9 1.3 %convolution_convert_fusion = bf16[128,16384]{1,0:T(8,128)(2,1)S(1)} fusion(bf16[16,16384]{1,0:T(8,128)(2,1)S(1)} %reshape.73, s32[128]{0:T(128)S(1)} %get-tuple-element.230), kind=kOutput, calls=%fused_computation.12 | convolution fusion | flops 69208064 | bytes 4719104 | tf_op jit(solution)/shard_map/dot_general | solution.py:107
  54.2 2.3 %copy.15 = bf16[16,8,8,2048]{3,2,0,1:T(8,128)(2,1)} copy(bf16[16,8,8,2048]{3,2,1,0:T(8,128)(2,1)S(1)} %bitcast.21) | data formatting | bytes 8388608 | tf_op jit(solution)/shard_map/reshape | solution.py:110
  56.5 9.2 %collective-permute-done.16 = bf16[127,2048]{1,0:T(8,128)(2,1)S(1)} collective-permute-done((bf16[127,2048]{1,0:T(8,128)(2,1)S(1)}, bf16[127,2048]{1,0:T(8,128)(2,1)S(1)}, u32[]{:S(2)}, u32[]{:S(2)}) %collective-permute-start.16) | collective-permute-done | bytes 520224 | tf_op jit(solution)/shard_map/ppermute | solution.py:11
  65.9 14.5 %while.16 = (s32[]{:T(128)}, f32[128,2048]{1,0:T(8,128)S(1)}, s32[]{:T(128)}, s32[128]{0:T(128)S(1)}, bf16[255,2048]{1,0:T(8,128)(2,1)S(1)}, /*index=5*/bf16[128...) while((s32[]{:T(128)}, f32[128,2048]{1,0:T(8,128)S(1)}, ...), condition=%wide.region_5.6_spmd.clone, body=%wide.region_4.5_spmd.clone.sunk | while | flops 3020168 | bytes 9454529 | solution.py:121
  66.0 1.1 %bitcast_convert_fusion.2 = f32[128,2048]{1,0:T(8,128)S(1)} fusion(bf16[128,8,2048]{2,0,1:T(8,128)(2,1)} %get-tuple-element.324, s32[]{:T(128)} %get-tuple-element.308), kind=kLoop, calls=%fused_computation.3.clone.1 | loop fusion | flops 262144 | bytes 1572868 | tf_op jit(solution)/shard_map/while/body/eval_jaxpr/convert_element_type | solution.py:118
  67.8 1.1 %bitcast_convert_fusion.2 = f32[128,2048]{1,0:T(8,128)S(1)} fusion(bf16[128,8,2048]{2,0,1:T(8,128)(2,1)} %get-tuple-element.324, s32[]{:T(128)} %get-tuple-element.308), kind=kLoop, calls=%fused_computation.3.clone.1 | loop fusion | flops 262144 | bytes 1572868 | tf_op jit(solution)/shard_map/while/body/eval_jaxpr/convert_element_type | solution.py:118
  69.7 1.1 %bitcast_convert_fusion.2 = f32[128,2048]{1,0:T(8,128)S(1)} fusion(bf16[128,8,2048]{2,0,1:T(8,128)(2,1)} %get-tuple-element.324, s32[]{:T(128)} %get-tuple-element.308), kind=kLoop, calls=%fused_computation.3.clone.1 | loop fusion | flops 262144 | bytes 1572868 | tf_op jit(solution)/shard_map/while/body/eval_jaxpr/convert_element_type | solution.py:118
  71.5 1.1 %bitcast_convert_fusion.2 = f32[128,2048]{1,0:T(8,128)S(1)} fusion(bf16[128,8,2048]{2,0,1:T(8,128)(2,1)} %get-tuple-element.324, s32[]{:T(128)} %get-tuple-element.308), kind=kLoop, calls=%fused_computation.3.clone.1 | loop fusion | flops 262144 | bytes 1572868 | tf_op jit(solution)/shard_map/while/body/eval_jaxpr/convert_element_type | solution.py:118
  73.3 1.1 %bitcast_convert_fusion.2 = f32[128,2048]{1,0:T(8,128)S(1)} fusion(bf16[128,8,2048]{2,0,1:T(8,128)(2,1)} %get-tuple-element.324, s32[]{:T(128)} %get-tuple-element.308), kind=kLoop, calls=%fused_computation.3.clone.1 | loop fusion | flops 262144 | bytes 1572868 | tf_op jit(solution)/shard_map/while/body/eval_jaxpr/convert_element_type | solution.py:118
  78.7 1.1 %bitcast_convert_fusion.2 = f32[128,2048]{1,0:T(8,128)S(1)} fusion(bf16[128,8,2048]{2,0,1:T(8,128)(2,1)} %get-tuple-element.324, s32[]{:T(128)} %get-tuple-element.308), kind=kLoop, calls=%fused_computation.3.clone.1 | loop fusion | flops 262144 | bytes 1572868 | tf_op jit(solution)/shard_map/while/body/eval_jaxpr/convert_element_type | solution.py:118
  80.4 7.2 %convolution_bitcast_fusion.1 = f32[16,8,1024]{2,1,0:T(8,128)S(1)} fusion(f32[128,2048]{1,0:T(8,128)S(1)} %get-tuple-element.181, f32[2048,1024]{1,0:T(8,128)} %constant.201.clone), kind=kOutput, calls=%fused_computation.17 | convolution fusion | flops 3221225472 | bytes 9961472 | tf_op jit(solution)/shard_map/dot_general | solution.py:123
  87.6 24.9 %all_to_all.5 = f32[16,8,1024]{2,1,0:T(8,128)S(1)} all-to-all(f32[16,8,1024]{2,1,0:T(8,128)S(1)} %convolution_bitcast_fusion.1), channel_id=1, replica_groups=mesh['tile'=32,'ir'=16] {'ir'}, dimensions={0} | all-to-all | bytes 1048576 | tf_op jit(solution)/shard_map/all_to_all | solution.py:21
  (110 shorter events, 16.5 us)
Async XLA Ops:
  0.0 10.1 %copy-start.1 = (bf16[8,1024]{1,0:T(8,128)(2,1)S(1)}, bf16[8,1024]{1,0:T(8,128)(2,1)}, u32[]{:S(2)}) copy-start(bf16[8,1024]{1,0:T(8,128)(2,1)} %param.8) | copy-start | bytes 49156
  0.8 9.2 %collective-permute-start = (bf16[1,1024]{1,0:T(2,128)(2,1)S(1)}, bf16[1,1024]{1,0:T(2,128)(2,1)S(1)}, u32[]{:S(2)}, u32[]{:S(2)}) collective-permute-start(bf16[1,1024]{1,0:T(2,128)(2,1)S(1)} %slice.49), channel_id=1, source_target_pairs={{0,1},{1,2},{2,3},{3,4},{4,5},{5,6},{6,7},{7,8},{8,9},{9,10},{10,1... | collective-permute-start | bytes 6152 | tf_op jit(solution)/shard_map/ppermute | solution.py:11
  6.9 11.2 %copy-start = (bf16[16,8,2,1024]{3,2,1,0:T(2,128)(2,1)S(1)}, bf16[16,8,2,1024]{3,2,1,0:T(2,128)(2,1)}, u32[]{:S(2)}) copy-start(bf16[16,8,2,1024]{3,2,1,0:T(2,128)(2,1)} %param.9) | copy-start | bytes 1572868
  10.0 42.8 %copy-start.2 = (s32[16]{0:T(128)S(1)}, s32[16]{0:T(128)}, u32[]{:S(2)}) copy-start(s32[16]{0:T(128)} %param.11) | copy-start | bytes 196
  13.0 5.9 %collective-permute-start.1 = (bf16[8,2048]{1,0:T(8,128)(2,1)S(1)}, bf16[8,2048]{1,0:T(8,128)(2,1)S(1)}, u32[]{:S(2)}, u32[]{:S(2)}) collective-permute-start(bf16[8,2048]{1,0:T(8,128)(2,1)S(1)} %get-tuple-element.249), channel_id=1, source_target_pairs={{0,1},{1,2},{2,3},{3,4},{4,5},{5,6},{6,7},{7,8},{8,9},{9,10},{10,1... | collective-permute-start | bytes 98312 | tf_op jit(solution)/shard_map/ppermute | solution.py:96
  13.0 6.0 %collective-permute-start.2 = (bf16[8,2048]{1,0:T(8,128)(2,1)S(1)}, bf16[8,2048]{1,0:T(8,128)(2,1)S(1)}, u32[]{:S(2)}, u32[]{:S(2)}) collective-permute-start(bf16[8,2048]{1,0:T(8,128)(2,1)S(1)} %get-tuple-element.249), channel_id=1, source_target_pairs={{0,15},{1,0},{2,1},{3,2},{4,3},{5,4},{6,5},{7,6},{8,7},{9,8},{10,9... | collective-permute-start | bytes 98312 | tf_op jit(solution)/shard_map/ppermute | solution.py:99
  18.9 4.6 %collective-permute-start.3 = (bf16[8,2048]{1,0:T(8,128)(2,1)S(1)}, bf16[8,2048]{1,0:T(8,128)(2,1)S(1)}, u32[]{:S(2)}, u32[]{:S(2)}) collective-permute-start(bf16[8,2048]{1,0:T(8,128)(2,1)S(1)} %collective-permute-done.1), channel_id=1, source_target_pairs={{0,1},{1,2},{2,3},{3,4},{4,5},{5,6},{6,7},{7,8},{8,9},{9,10},{10,1... | collective-permute-start | bytes 98312 | tf_op jit(solution)/shard_map/ppermute | solution.py:96
  19.0 4.6 %collective-permute-start.4 = (bf16[8,2048]{1,0:T(8,128)(2,1)S(1)}, bf16[8,2048]{1,0:T(8,128)(2,1)S(1)}, u32[]{:S(2)}, u32[]{:S(2)}) collective-permute-start(bf16[8,2048]{1,0:T(8,128)(2,1)S(1)} %collective-permute-done.2), channel_id=1, source_target_pairs={{0,15},{1,0},{2,1},{3,2},{4,3},{5,4},{6,5},{7,6},{8,7},{9,8},{10,9... | collective-permute-start | bytes 98312 | tf_op jit(solution)/shard_map/ppermute | solution.py:99
  23.4 4.6 %collective-permute-start.5 = (bf16[8,2048]{1,0:T(8,128)(2,1)S(1)}, bf16[8,2048]{1,0:T(8,128)(2,1)S(1)}, u32[]{:S(2)}, u32[]{:S(2)}) collective-permute-start(bf16[8,2048]{1,0:T(8,128)(2,1)S(1)} %collective-permute-done.3), channel_id=1, source_target_pairs={{0,1},{1,2},{2,3},{3,4},{4,5},{5,6},{6,7},{7,8},{8,9},{9,10},{10,1... | collective-permute-start | bytes 98312 | tf_op jit(solution)/shard_map/ppermute | solution.py:96
  23.6 4.6 %collective-permute-start.6 = (bf16[8,2048]{1,0:T(8,128)(2,1)S(1)}, bf16[8,2048]{1,0:T(8,128)(2,1)S(1)}, u32[]{:S(2)}, u32[]{:S(2)}) collective-permute-start(bf16[8,2048]{1,0:T(8,128)(2,1)S(1)} %collective-permute-done.4), channel_id=1, source_target_pairs={{0,15},{1,0},{2,1},{3,2},{4,3},{5,4},{6,5},{7,6},{8,7},{9,8},{10,9... | collective-permute-start | bytes 98312 | tf_op jit(solution)/shard_map/ppermute | solution.py:99
  28.0 4.6 %collective-permute-start.7 = (bf16[8,2048]{1,0:T(8,128)(2,1)S(1)}, bf16[8,2048]{1,0:T(8,128)(2,1)S(1)}, u32[]{:S(2)}, u32[]{:S(2)}) collective-permute-start(bf16[8,2048]{1,0:T(8,128)(2,1)S(1)} %collective-permute-done.5), channel_id=1, source_target_pairs={{0,1},{1,2},{2,3},{3,4},{4,5},{5,6},{6,7},{7,8},{8,9},{9,10},{10,1... | collective-permute-start | bytes 98312 | tf_op jit(solution)/shard_map/ppermute | solution.py:96
  28.1 4.6 %collective-permute-start.8 = (bf16[8,2048]{1,0:T(8,128)(2,1)S(1)}, bf16[8,2048]{1,0:T(8,128)(2,1)S(1)}, u32[]{:S(2)}, u32[]{:S(2)}) collective-permute-start(bf16[8,2048]{1,0:T(8,128)(2,1)S(1)} %collective-permute-done.6), channel_id=1, source_target_pairs={{0,15},{1,0},{2,1},{3,2},{4,3},{5,4},{6,5},{7,6},{8,7},{9,8},{10,9... | collective-permute-start | bytes 98312 | tf_op jit(solution)/shard_map/ppermute | solution.py:99
  32.5 4.6 %collective-permute-start.9 = (bf16[8,2048]{1,0:T(8,128)(2,1)S(1)}, bf16[8,2048]{1,0:T(8,128)(2,1)S(1)}, u32[]{:S(2)}, u32[]{:S(2)}) collective-permute-start(bf16[8,2048]{1,0:T(8,128)(2,1)S(1)} %collective-permute-done.7), channel_id=1, source_target_pairs={{0,1},{1,2},{2,3},{3,4},{4,5},{5,6},{6,7},{7,8},{8,9},{9,10},{10,1... | collective-permute-start | bytes 98312 | tf_op jit(solution)/shard_map/ppermute | solution.py:96
  32.7 4.6 %collective-permute-start.10 = (bf16[8,2048]{1,0:T(8,128)(2,1)S(1)}, bf16[8,2048]{1,0:T(8,128)(2,1)S(1)}, u32[]{:S(2)}, u32[]{:S(2)}) collective-permute-start(bf16[8,2048]{1,0:T(8,128)(2,1)S(1)} %collective-permute-done.8), channel_id=1, source_target_pairs={{0,15},{1,0},{2,1},{3,2},{4,3},{5,4},{6,5},{7,6},{8,7},{9,8},{10,9... | collective-permute-start | bytes 98312 | tf_op jit(solution)/shard_map/ppermute | solution.py:99
  37.1 4.6 %collective-permute-start.11 = (bf16[8,2048]{1,0:T(8,128)(2,1)S(1)}, bf16[8,2048]{1,0:T(8,128)(2,1)S(1)}, u32[]{:S(2)}, u32[]{:S(2)}) collective-permute-start(bf16[8,2048]{1,0:T(8,128)(2,1)S(1)} %collective-permute-done.9), channel_id=1, source_target_pairs={{0,1},{1,2},{2,3},{3,4},{4,5},{5,6},{6,7},{7,8},{8,9},{9,10},{10,1... | collective-permute-start | bytes 98312 | tf_op jit(solution)/shard_map/ppermute | solution.py:96
  37.2 4.6 %collective-permute-start.12 = (bf16[8,2048]{1,0:T(8,128)(2,1)S(1)}, bf16[8,2048]{1,0:T(8,128)(2,1)S(1)}, u32[]{:S(2)}, u32[]{:S(2)}) collective-permute-start(bf16[8,2048]{1,0:T(8,128)(2,1)S(1)} %collective-permute-done.10), channel_id=1, source_target_pairs={{0,15},{1,0},{2,1},{3,2},{4,3},{5,4},{6,5},{7,6},{8,7},{9,8},{10,9... | collective-permute-start | bytes 98312 | tf_op jit(solution)/shard_map/ppermute | solution.py:99
  41.6 4.6 %collective-permute-start.13 = (bf16[8,2048]{1,0:T(8,128)(2,1)S(1)}, bf16[8,2048]{1,0:T(8,128)(2,1)S(1)}, u32[]{:S(2)}, u32[]{:S(2)}) collective-permute-start(bf16[8,2048]{1,0:T(8,128)(2,1)S(1)} %collective-permute-done.11), channel_id=1, source_target_pairs={{0,1},{1,2},{2,3},{3,4},{4,5},{5,6},{6,7},{7,8},{8,9},{9,10},{10,1... | collective-permute-start | bytes 98312 | tf_op jit(solution)/shard_map/ppermute | solution.py:96
  41.8 4.6 %collective-permute-start.14 = (bf16[8,2048]{1,0:T(8,128)(2,1)S(1)}, bf16[8,2048]{1,0:T(8,128)(2,1)S(1)}, u32[]{:S(2)}, u32[]{:S(2)}) collective-permute-start(bf16[8,2048]{1,0:T(8,128)(2,1)S(1)} %collective-permute-done.12), channel_id=1, source_target_pairs={{0,15},{1,0},{2,1},{3,2},{4,3},{5,4},{6,5},{7,6},{8,7},{9,8},{10,9... | collective-permute-start | bytes 98312 | tf_op jit(solution)/shard_map/ppermute | solution.py:99
  46.2 4.6 %collective-permute-start.15 = (bf16[8,2048]{1,0:T(8,128)(2,1)S(1)}, bf16[8,2048]{1,0:T(8,128)(2,1)S(1)}, u32[]{:S(2)}, u32[]{:S(2)}) collective-permute-start(bf16[8,2048]{1,0:T(8,128)(2,1)S(1)} %collective-permute-done.13), channel_id=1, source_target_pairs={{0,1},{1,2},{2,3},{3,4},{4,5},{5,6},{6,7},{7,8},{8,9},{9,10},{10,1... | collective-permute-start | bytes 98312 | tf_op jit(solution)/shard_map/ppermute | solution.py:96
  50.9 14.8 %collective-permute-start.16 = (bf16[127,2048]{1,0:T(8,128)(2,1)S(1)}, bf16[127,2048]{1,0:T(8,128)(2,1)S(1)}, u32[]{:S(2)}, u32[]{:S(2)}) collective-permute-start(bf16[127,2048]{1,0:T(8,128)(2,1)S(1)} %slice.62), channel_id=1, source_target_pairs={{0,16},{16,32},{32,48},{48,64},{64,80},{80,96},{96,112},{112,128},... | collective-permute-start | bytes 1560584 | tf_op jit(solution)/shard_map/ppermute | solution.py:11
